TPU v7x, 256 devices: a whole 4x4x8 slice. The times are simulated.
256 devices in a mesh: dp: 8 (over x, core), seq: 32 (over z, y).
Axes of the slice: x: 4, y: 4, z: 8, core: 2. Of those that a mesh axis runs over, the one named last changes fastest.
Arguments:
- queries: bfloat16 [8, 8192, 2048], P('dp', 'seq'), may hold values from -40 to 40
- keys: bfloat16 [8, 8192, 2048], P('dp', 'seq'), may hold values from -40 to 40
- values: bfloat16 [8, 8192, 2048], P('dp', 'seq'), may hold values from -6 to 6
- key_gain: float32 [2048], replicated, may hold values from 0.25 to 1.75
- random_blocks: int32 [16, 128, 3], P(None, 'seq'), may hold values from 2 to 127, as said below
- out_grad: bfloat16 [8, 8192, 2048], P('dp', 'seq'), may hold values from -6 to 6
Outputs:
- attended: bfloat16 [8, 8192, 2048], P('dp', 'seq')
- query_grad: bfloat16 [8, 8192, 2048], P('dp', 'seq')
- key_grad: bfloat16 [8, 8192, 2048], P('dp', 'seq')
- value_grad: bfloat16 [8, 8192, 2048], P('dp', 'seq')
- gain_grad: float32 [2048], replicated
Inputs may be any that keep to these rules, and one draw needn't show every extreme that they name: `random_blocks`: for the 4 query blocks of one device, all heads and entries together, at most 9 entries name blocks held by any one device (blocks d * 4 to d * 4 + 3), and exactly 9 name the blocks of some device.
All inputs are finite; a program needn't handle non-finite values.
Results may differ from a plain program's by a relative error of at most 0.03.
The roundings to bfloat16 on the way count: a program that leaves them out, or rounds other values in their place, can miss the bound.
Values may be sent and summed in bfloat16 or wider, within the bound.
No kernel may reach another device: no remote copies, remote signals or barrier semaphores. Data moves between devices by JAX's collectives and lax.ppermute only.
A program may use at most 128 MiB of HBM per device.

v0:
```python
import math
import jax
import jax.numpy as jnp
from jax import lax
from jax.sharding import PartitionSpec as P

HEADS = 16
HD = 128
BLOCK = 64
NG = 2
NR = 3
NK = 8
NEGATIVE = -1e30


def broadcast(block, axis, owner):
    block = jnp.where(lax.axis_index(axis) == owner, block, jnp.zeros_like(block))
    return lax.psum(block, axis)


def padded_2(cells, sides, width):
    for axis, dim in sides:
        count = lax.axis_size(axis)
        ends = count - 1
        head = lax.slice_in_dim(cells, 0, width, axis=dim)
        tail = lax.slice_in_dim(cells, cells.shape[dim] - width, cells.shape[dim], axis=dim)
        cells = jnp.concatenate(
            [
                lax.ppermute(tail, axis, [(i, (i + 1) % count) for i in range(ends)]),
                cells,
                lax.ppermute(head, axis, [((i + 1) % count, i) for i in range(ends)]),
            ],
            axis=dim,
        )
    return cells


def passed_along(array, axis, by):
    length = lax.axis_size(axis)
    pairs = [(i, i + by) for i in range(length) if 0 <= i + by < length]
    return lax.ppermute(array, axis, pairs)


def to_heads(rows_in):
    return rows_in.reshape(rows_in.shape[0] // BLOCK, BLOCK, HEADS, HD).transpose(2, 0, 1, 3)


def from_heads(blocks_in):
    return blocks_in.transpose(1, 2, 0, 3).reshape(1, blocks_in.shape[1] * BLOCK, HEADS * HD)


def build_list(edge_part, window_part, random_in):
    head_count = random_in.shape[0]
    block_count = random_in.shape[1]
    global_list = jnp.broadcast_to(
        edge_part[:, None], (head_count, block_count) + edge_part.shape[1:]
    )
    window_list = jnp.stack(
        [window_part[:, offset : offset + block_count] for offset in range(3)], axis=2
    )
    joined = jnp.concatenate([global_list, window_list, random_in], axis=2)
    return joined.reshape(head_count, block_count, NK * BLOCK, HD)


def spread_terms(coef, rows_in):
    head_count = rows_in.shape[0]
    block_count = rows_in.shape[1]
    coef_blocks = coef.reshape(head_count, block_count, BLOCK, NK, BLOCK)
    global_term = jnp.einsum(
        "hpbgc,hpbd->hgcd", coef_blocks[:, :, :, :NG], rows_in, preferred_element_type=jnp.float32
    )
    padded = jnp.zeros((head_count, block_count + 2, BLOCK, HD), jnp.float32)
    for offset in range(3):
        term = jnp.einsum(
            "hpbc,hpbd->hpcd",
            coef_blocks[:, :, :, NG + offset],
            rows_in,
            preferred_element_type=jnp.float32,
        )
        padded = padded + jnp.pad(term, ((0, 0), (offset, 2 - offset), (0, 0), (0, 0)))
    random_term = jnp.einsum(
        "hpbrc,hpbd->hprcd",
        coef_blocks[:, :, :, NG + 3 :],
        rows_in,
        preferred_element_type=jnp.float32,
    )
    return (global_term, padded, random_term)


def sparse_group(
    query_blk,
    edge_key,
    edge_value,
    window_key,
    window_value,
    random_key,
    random_value,
    grad_blk,
    valid_keys,
    keep_rows,
):
    score_scale = HD ** (-0.5)
    key_list = build_list(edge_key, window_key, random_key)
    value_list = build_list(edge_value, window_value, random_value)
    key_mask = jnp.repeat(valid_keys, BLOCK, axis=1)[None, :, None, :]
    scores = (
        jnp.einsum("hpbd,hpnd->hpbn", query_blk, key_list, preferred_element_type=jnp.float32)
        * score_scale
    )
    scores = jnp.where(key_mask, scores, NEGATIVE)
    row_top = jnp.max(scores, axis=3, keepdims=True)
    expo_vals = jnp.where(key_mask, jnp.exp(scores - row_top), 0.0)
    row_total = jnp.sum(expo_vals, axis=3, keepdims=True)
    numerator = jnp.einsum(
        "hpbn,hpnd->hpbd",
        expo_vals.astype(jnp.bfloat16),
        value_list,
        preferred_element_type=jnp.float32,
    )
    attended = (numerator / row_total).astype(jnp.bfloat16)
    row_delta = jnp.sum(grad_blk.astype(jnp.float32) * attended.astype(jnp.float32), axis=3)
    weights = expo_vals / row_total * keep_rows[None, :, None, None]
    dprobs = jnp.einsum("hpbd,hpnd->hpbn", grad_blk, value_list, preferred_element_type=jnp.float32)
    dscores = (weights * (dprobs - row_delta[:, :, :, None]) * score_scale).astype(jnp.bfloat16)
    dquery = jnp.einsum("hpbn,hpnd->hpbd", dscores, key_list, preferred_element_type=jnp.float32)
    key_global, key_padded, key_random = spread_terms(dscores, query_blk)
    value_global, value_padded, value_random = spread_terms(weights.astype(jnp.bfloat16), grad_blk)
    global_part = jnp.stack([key_global, value_global], axis=1)
    padded = jnp.stack([key_padded, value_padded], axis=1)
    random_part = jnp.stack([key_random, value_random], axis=1)
    return (attended, dquery, global_part, padded, random_part)


def shards(queries, keys, values, key_gain, random_blocks, out_grad):
    score_scale = HD ** (-0.5)
    tok_count = queries.shape[1]
    per_dev = tok_count // BLOCK
    owners = lax.axis_size("seq")
    seq_place = lax.axis_index("seq")
    total_blocks = owners * per_dev
    first_block = seq_place * per_dev
    key_eff = (keys[0].astype(jnp.float32) * key_gain).astype(jnp.bfloat16)
    edge_count = NG * BLOCK
    edge_rows = broadcast(
        jnp.stack(
            [
                queries[0, :edge_count],
                key_eff[:edge_count],
                values[0, :edge_count],
                out_grad[0, :edge_count],
            ]
        ),
        "seq",
        0,
    )
    window_rows = padded_2(jnp.stack([key_eff, values[0]]), (("seq", 1),), BLOCK)
    query_h = to_heads(queries[0])
    key_h = to_heads(key_eff)
    value_h = to_heads(values[0])
    grad_h = to_heads(out_grad[0])
    edge_heads = [to_heads(edge_rows[slot_pick]) for slot_pick in range(4)]
    window_key = to_heads(window_rows[0])
    window_value = to_heads(window_rows[1])
    request_count = HEADS * per_dev * NR
    capacity = (request_count + owners - 1) // owners + 3
    target = random_blocks.reshape(request_count)
    owner_dev = target // per_dev
    table_index = (
        jnp.arange(request_count, dtype=jnp.int32) // (per_dev * NR) * per_dev + target % per_dev
    )
    onehot = (owner_dev[:, None] == jnp.arange(owners, dtype=jnp.int32)[None, :]).astype(jnp.int32)
    before = jnp.cumsum(onehot, axis=0) - onehot
    slot_rank = jnp.sum(before * onehot, axis=1)
    position = owner_dev * capacity + slot_rank
    outgoing = (
        jnp.full((owners * capacity,), -1, jnp.int32)
        .at[position]
        .set(table_index)
        .reshape(owners, capacity)
    )
    kv_table = jnp.concatenate([key_h, value_h], axis=3).reshape(HEADS * per_dev, BLOCK, 2 * HD)
    index_part = lax.all_to_all(outgoing, "seq", split_axis=0, concat_axis=0, tiled=True)
    picked = kv_table[jnp.clip(index_part, 0, HEADS * per_dev - 1)]
    fetch_result = (
        lax.all_to_all(picked, "seq", split_axis=0, concat_axis=0, tiled=True),
        index_part,
    )
    arrived, served = fetch_result
    fetched = arrived.reshape(owners * capacity, BLOCK, 2 * HD)[position].reshape(
        HEADS, per_dev, NR, BLOCK, 2 * HD
    )
    fetched_key = fetched[..., :HD]
    fetched_value = fetched[..., HD:]
    block_index = first_block + jnp.arange(per_dev, dtype=jnp.int32)
    window_index = block_index[:, None] + jnp.arange(-1, 2, dtype=jnp.int32)[None, :]
    valid_keys = jnp.concatenate(
        [
            jnp.ones((per_dev, NG), bool),
            (window_index >= NG) & (window_index < total_blocks),
            jnp.ones((per_dev, NR), bool),
        ],
        axis=1,
    )
    keep_rows = (block_index >= NG).astype(jnp.float32)
    group_size = math.gcd(HEADS, 4)

    def by_group(array_in):
        return array_in.reshape((HEADS // group_size, group_size) + array_in.shape[1:])

    def merge_groups(array_in):
        return array_in.reshape((HEADS,) + array_in.shape[2:])

    def run_group(bundle):
        return sparse_group(
            bundle[0],
            bundle[1],
            bundle[2],
            bundle[3],
            bundle[4],
            bundle[5],
            bundle[6],
            bundle[7],
            valid_keys,
            keep_rows,
        )

    grouped = lax.map(
        run_group,
        (
            by_group(query_h),
            by_group(edge_heads[1]),
            by_group(edge_heads[2]),
            by_group(window_key),
            by_group(window_value),
            by_group(fetched_key),
            by_group(fetched_value),
            by_group(grad_h),
        ),
    )
    attended_h, dquery_h, global_part, padded, random_part = [
        merge_groups(piece_out) for piece_out in grouped
    ]
    edge_query = edge_heads[0].reshape(HEADS, edge_count, HD)
    edge_grad = edge_heads[3].reshape(HEADS, edge_count, HD)
    flat_key = key_h.reshape(HEADS, tok_count, HD)
    flat_value = value_h.reshape(HEADS, tok_count, HD)
    edge_scores = (
        jnp.einsum("hqd,htd->hqt", edge_query, flat_key, preferred_element_type=jnp.float32)
        * score_scale
    )
    edge_top = lax.pmax(jnp.max(edge_scores, axis=2), "seq")
    edge_expo = jnp.exp(edge_scores - edge_top[:, :, None])
    edge_total, edge_numer = lax.psum(
        (
            jnp.sum(edge_expo, axis=2),
            jnp.einsum(
                "hqt,htd->hqd",
                edge_expo.astype(jnp.bfloat16),
                flat_value,
                preferred_element_type=jnp.float32,
            ),
        ),
        "seq",
    )
    edge_out = (edge_numer / edge_total[:, :, None]).astype(jnp.bfloat16)
    edge_delta = jnp.sum(edge_grad.astype(jnp.float32) * edge_out.astype(jnp.float32), axis=2)
    edge_weights = edge_expo / edge_total[:, :, None]
    edge_dprobs = jnp.einsum(
        "hqd,htd->hqt", edge_grad, flat_value, preferred_element_type=jnp.float32
    )
    edge_dscores = (edge_weights * (edge_dprobs - edge_delta[:, :, None]) * score_scale).astype(
        jnp.bfloat16
    )
    edge_dquery = jnp.einsum(
        "hqt,htd->hqd", edge_dscores, flat_key, preferred_element_type=jnp.float32
    )
    local_dkey = jnp.einsum(
        "hqt,hqd->htd", edge_dscores, edge_query, preferred_element_type=jnp.float32
    )
    local_dvalue = jnp.einsum(
        "hqt,hqd->htd",
        edge_weights.astype(jnp.bfloat16),
        edge_grad,
        preferred_element_type=jnp.float32,
    )
    random_rounded = (
        random_part.transpose(0, 2, 3, 4, 1, 5)
        .reshape(request_count, BLOCK, 2 * HD)
        .astype(jnp.bfloat16)
    )
    sendback = (
        jnp.zeros((owners * capacity, BLOCK, 2 * HD), jnp.bfloat16)
        .at[position]
        .set(random_rounded)
        .reshape(owners, capacity, BLOCK, 2 * HD)
    )
    returned = lax.all_to_all(sendback, "seq", split_axis=0, concat_axis=0, tiled=True)
    owner_table = (
        served.reshape(1, owners * capacity)
        == jnp.arange(HEADS * per_dev, dtype=jnp.int32)[:, None]
    ).astype(jnp.bfloat16)
    summed = jnp.dot(
        owner_table,
        returned.reshape(owners * capacity, BLOCK * 2 * HD),
        preferred_element_type=jnp.float32,
    )
    summed = summed.reshape(HEADS, per_dev, BLOCK, 2, HD).transpose(0, 3, 1, 2, 4)
    from_right = passed_along(padded[:, :, 0].astype(jnp.bfloat16), "seq", -1).astype(jnp.float32)
    from_left = passed_along(padded[:, :, per_dev + 1].astype(jnp.bfloat16), "seq", 1).astype(
        jnp.float32
    )
    edge_dquery_sum, global_sum = lax.psum((edge_dquery, global_part), "seq")
    accum = padded[:, :, 1 : per_dev + 1]
    accum = accum + jnp.stack([local_dkey, local_dvalue], axis=1).reshape(
        HEADS, 2, per_dev, BLOCK, HD
    )
    accum = accum + summed
    accum = accum.at[:, :, per_dev - 1].add(from_right)
    accum = accum.at[:, :, 0].add(from_left)
    is_first = (seq_place == 0).astype(jnp.float32)
    accum = accum.at[:, :, :NG].add(global_sum * is_first)
    is_edge = (block_index < NG)[None, :, None, None]
    tail_zeros = jnp.zeros((HEADS, per_dev - NG, BLOCK, HD), jnp.float32)
    edge_dq_blocks = jnp.concatenate(
        [edge_dquery_sum.reshape(HEADS, NG, BLOCK, HD), tail_zeros], axis=1
    )
    edge_out_blocks = jnp.concatenate(
        [edge_out.reshape(HEADS, NG, BLOCK, HD), tail_zeros.astype(jnp.bfloat16)], axis=1
    )
    dquery_all = jnp.where(is_edge, edge_dq_blocks, dquery_h).astype(jnp.bfloat16)
    attended_all = jnp.where(is_edge, edge_out_blocks, attended_h)
    key_eff_grad = accum[:, 0]
    gain_heads = key_gain.reshape(HEADS, HD)
    key_grad_h = (key_eff_grad * gain_heads[:, None, None, :]).astype(jnp.bfloat16)
    value_grad_h = accum[:, 1].astype(jnp.bfloat16)
    gain_term = jnp.sum(key_eff_grad * to_heads(keys[0]).astype(jnp.float32), axis=(1, 2)).reshape(
        HEADS * HD
    )
    gain_grad = lax.psum(gain_term, ("dp", "seq"))
    return (
        from_heads(attended_all),
        from_heads(dquery_all),
        from_heads(key_grad_h),
        from_heads(value_grad_h),
        gain_grad,
    )


def solution(mesh):
    placed = (
        P("dp", "seq", None),
        P("dp", "seq", None),
        P("dp", "seq", None),
        P(),
        P(None, "seq", None),
        P("dp", "seq", None),
    )
    return jax.shard_map(
        shards,
        mesh=mesh,
        in_specs=placed,
        out_specs=(
            P("dp", "seq", None),
            P("dp", "seq", None),
            P("dp", "seq", None),
            P("dp", "seq", None),
            P(),
        ),
        check_vma=False,
    )
```

profile of v0, /device:TPU:1, one launch (start us, length us, event | category | flops | bytes accessed | tf_op | source)
XLA Modules:
  0.0 1441.6 jit_solution(389370633972243564)
XLA Ops:
  11.2 12.0 all-to-all-start
  33.7 10.3 gather_fusion
  43.9 7.5 all-to-all-start.1
  68.2 25.1 %collective-permute-done = bf16[2,64,2048]{2,1,0:T(8,128)(2,1)} collective-permute-done((bf16[2,64,2048]{2,1,0:T(8,128)(2,1)}, bf16[2,64,2048]{2,1,0:T(8,128)(2,1)}, u32[]{:S(2)}, u32[]{:S(2)}) %collective-permute-start) | collective-permute-done | bytes 524320 | tf_op jit(solution)/shard_map/ppermute | solution.py:29
  93.3 21.3 %collective-permute-done.1 = bf16[2,64,2048]{2,1,0:T(8,128)(2,1)} collective-permute-done((bf16[2,64,2048]{2,1,0:T(8,128)(2,1)}, bf16[2,64,2048]{2,1,0:T(8,128)(2,1)}, u32[]{:S(2)}, u32[]{:S(2)}) %collective-permute-start.1) | collective-permute-done | bytes 524320 | tf_op jit(solution)/shard_map/ppermute | solution.py:31
  119.1 206.0 %all-reduce.14.cloned.1.call-done = bf16[4,128,2048]{2,1,0:T(8,128)(2,1)} async-done(((bf16[4,128,2048]{2,1,0:T(8,128)(2,1)}), bf16[4,128,2048]{2,1,0:T(8,128)(2,1)}) %all-reduce.14.cloned.1.call-update) | async-done | bytes 2097168 | tf_op jit(solution)/shard_map/psum | solution.py:18
  329.1 11.8 gather_fusion.1
  340.9 8.0 fusion.134
  348.9 287.8 %while.24 = (s32[]{:T(128)}, bf16[4,4,4,64,128]{4,3,2,1,0:T(8,128)(2,1)}, bf16[4,4,4,64,128]{4,3,2,1,0:T(8,128)(2,1)}, f32[4,4,2,2,64,128]{5,1,0,2,4,3:T(4,128)}...) while((s32[]{:T(128)}, ...), condition=%wide.region_14.15_spmd.clone, body=%wide.region_10.14_spmd.clone.sunk | while | flops 952370176 | bytes 142396560 | solution.py:227
  368.6 5.1 bitcast_dynamic-update-slice_fusion.6
  440.4 5.1 bitcast_dynamic-update-slice_fusion.6
  584.1 5.1 bitcast_dynamic-update-slice_fusion.6
  636.7 12.7 copy.168
  649.4 10.8 reshape.529
  665.1 29.1 %scatter_fusion = bf16[288,64,256]{2,1,0:T(8,128)(2,1)} fusion(bf16[288,64,256]{2,1,0:T(8,128)(2,1)} %broadcast_in_dim.167, s32[192]{0:T(256)S(1)} %bitcast.511, bf16[192,64,256]{2,1,0:T(8,128)(2,1)} %reshape.529), kind=kCustom, calls=%fused_computation.3 | custom fusion | bytes 18875136 | tf_op jit(solution)/shard_map/scatter | solution.py:294
  694.3 6.0 all-to-all-start.2
  704.3 248.7 %pmax.7 = f32[16,128]{1,0:T(8,128)S(1)} all-reduce(f32[16,128]{1,0:T(8,128)S(1)} %get-tuple-element.352), channel_id=1, replica_groups=mesh['dp'=8,'seq'=32] {'seq'}, use_global_device_ids=true, to_apply=%region_2.3 | all-reduce | flops 2048 | bytes 16384 | tf_op jit(solution)/shard_map/pmax | solution.py:251
  960.4 59.2 %psum.44 = f32[16,128]{1,0:T(8,128)S(1)} all-reduce(f32[16,128]{1,0:T(8,128)S(1)} %fusion.95), channel_id=1, replica_groups=mesh['dp'=8,'seq'=32] {'seq'}, use_global_device_ids=true, to_apply=%region_5.6 | all-reduce | flops 2048 | bytes 16384 | tf_op jit(solution)/shard_map/psum | solution.py:253
  1033.0 99.2 %all-reduce.16.cloned.1.call-done = (f32[16,128,128]{2,1,0:T(8,128)}, f32[16,2,2,64,128]{4,0,1,3,2:T(8,128)}) async-done(((f32[16,128,128]{2,1,0:T(8,128)}, f32[16,2,2,64,128]{4,0,1,3,2:T(8,128)}), (f32[16,128,128]{2,1,0:T(8,128)}, f32[16,2,2,64,128]{4,0,1,3,2:T(8,128)})) %all-reduce.16.cloned.1.call-update) | async-done | bytes 3145744 | tf_op jit(solution)/shard_map/psum | solution.py:253
  1141.9 123.4 %all-reduce.17 = bf16[16,2,64,128]{3,2,1,0:T(8,128)(2,1)S(1)} all-reduce(f32[16,2,64,128]{3,2,1,0:T(8,128)} %bitcast.485), channel_id=1, replica_groups=mesh['dp'=8,'seq'=32] {'seq'}, use_global_device_ids=true, to_apply=%region_16.17 | all-reduce | flops 262144 | bytes 1572864 | tf_op jit(solution)/shard_map/psum | solution.py:312
  1273.5 18.5 %copy.212 = bf16[36,8,64,256]{3,1,2,0:T(8,128)(2,1)} copy(bf16[36,8,64,256]{3,2,1,0:T(8,128)(2,1)} %bitcast.182) | data formatting | bytes 18874368
  1292.0 16.1 %dot_general.116 = bf16[64,2,128,288]{2,1,0,3:T(2,128)(2,1)} reshape(bf16[16384,288]{0,1:T(8,128)(2,1)} %bitcast.460) | data formatting | bytes 18874368 | tf_op jit(solution)/shard_map/dot_general | solution.py:302
  1308.1 12.3 fusion.85
  1328.3 106.2 %psum.47 = f32[2048]{0:T(1024)} all-reduce(f32[2048]{0:T(1024)S(1)} %bitcast.508), channel_id=1, replica_groups=mesh['dp'=8,'seq'=32] {'dp','seq'}, use_global_device_ids=true, to_apply=%region_20.21 | all-reduce | flops 2048 | bytes 16384 | tf_op jit(solution)/shard_map/psum | solution.py:339
  (477 shorter events, 365.1 us)
Async XLA Ops:
  9.3 58.8 %copy-start.31 = (s32[192,1]{0,1:T(1,128)}, s32[192,1]{0,1:T(1,128)S(1)}, u32[]{:S(2)}) copy-start(s32[192,1]{0,1:T(1,128)S(1)} %compare_select_fusion.1) | copy-start | bytes 2308
  11.2 20.6 %all-to-all-start = ((s32[32,1,9]{2,1,0:T(1,128)}), s32[32,1,9]{2,1,0:T(1,128)S(1)}, u32[]{:S(2)}, u32[]{:S(2)}) async-start(s32[32,1,9]{2,1,0:T(1,128)} %bitcast.20), calls=%async_computation | async-start | bytes 32768 | tf_op jit(solution)/shard_map/all_to_all | solution.py:182
  43.9 285.2 %all-to-all-start.1 = ((bf16[32,9,64,256]{3,2,1,0:T(8,128)(2,1)}), bf16[32,9,64,256]{3,2,1,0:T(8,128)(2,1)}, u32[]{:S(2)}, u32[]{:S(2)}) async-start(bf16[32,9,64,256]{3,2,1,0:T(8,128)(2,1)} %bitcast.459), calls=%async_computation.1 | async-start | bytes 18874368 | tf_op jit(solution)/shard_map/all_to_all | solution.py:185
  51.4 273.7 %all-reduce.14.cloned.1.call-start = ((), (), s32[]{:S(2)}) async-start(), calls=%async_computation.3 | async-start | bytes 4194304 | tf_op jit(solution)/shard_map/psum | solution.py:18
  58.0 35.3 %collective-permute-start = (bf16[2,64,2048]{2,1,0:T(8,128)(2,1)}, bf16[2,64,2048]{2,1,0:T(8,128)(2,1)}, u32[]{:S(2)}, u32[]{:S(2)}) collective-permute-start(bf16[2,64,2048]{2,1,0:T(8,128)(2,1)} %get-tuple-element.342), channel_id=1, source_target_pairs={{0,1},{1,2},{2,3},{3,4},{4,5},{5,6},{6,7},{7,8},{8,9},{9,10},{10,1... | collective-permute-start | bytes 1572872 | tf_op jit(solution)/shard_map/ppermute | solution.py:29
  61.8 52.8 %collective-permute-start.1 = (bf16[2,64,2048]{2,1,0:T(8,128)(2,1)}, bf16[2,64,2048]{2,1,0:T(8,128)(2,1)}, u32[]{:S(2)}, u32[]{:S(2)}) collective-permute-start(bf16[2,64,2048]{2,1,0:T(8,128)(2,1)} %get-tuple-element.343), channel_id=1, source_target_pairs={{1,0},{2,1},{3,2},{4,3},{5,4},{6,5},{7,6},{8,7},{9,8},{10,9},{11,1... | collective-permute-start | bytes 1572872 | tf_op jit(solution)/shard_map/ppermute | solution.py:31
  355.9 3.7 copy-start.1
  380.2 3.8 copy-start.5
  427.7 3.7 copy-start.1
  452.0 3.8 copy-start.5
  499.5 3.7 copy-start.1
  523.8 3.8 copy-start.5
  526.0 3.0 copy-start
  571.3 3.7 copy-start.1
  595.6 3.8 copy-start.5
  660.3 4.9 copy-start.32
  694.3 6.1 copy-start.7
  694.3 6.1 copy-start.29
  694.3 579.3 %all-to-all-start.2 = ((bf16[32,9,64,256]{3,2,1,0:T(8,128)(2,1)}), bf16[32,9,64,256]{3,2,1,0:T(8,128)(2,1)}, u32[]{:S(2)}, u32[]{:S(2)}) async-start(bf16[32,9,64,256]{3,2,1,0:T(8,128)(2,1)} %bitcast.457), calls=%async_computation.2 | async-start | bytes 18874368 | tf_op jit(solution)/shard_map/all_to_all | solution.py:297
  700.3 432.0 %all-reduce.16.cloned.1.call-start = ((), (), s32[]{:S(2)}) async-start(), calls=%async_computation.4 | async-start | bytes 6291456 | tf_op jit(solution)/shard_map/psum | solution.py:253
  1019.5 5.5 slice-start.1
  1019.5 5.5 slice-start.2
  1026.9 293.5 %collective-permute-start.2 = (bf16[16,2,64,128]{3,0,1,2:T(8,128)(2,1)}, bf16[16,2,64,128]{3,0,1,2:T(8,128)(2,1)}, u32[]{:S(2)}, u32[]{:S(2)}) collective-permute-start(bf16[16,2,64,128]{3,0,1,2:T(8,128)(2,1)} %get-tuple-element.335), channel_id=1, source_target_pairs={{1,0},{2,1},{3,2},{4,3},{5,4},{6,5},{7,6},{8,7},{9,8},{10,9},{11,1... | collective-permute-start | bytes 1572872 | tf_op jit(solution)/shard_map/ppermute | solution.py:41
  1028.2 293.7 %collective-permute-start.3 = (bf16[16,2,64,128]{3,0,1,2:T(8,128)(2,1)}, bf16[16,2,64,128]{3,0,1,2:T(8,128)(2,1)}, u32[]{:S(2)}, u32[]{:S(2)}) collective-permute-start(bf16[16,2,64,128]{3,0,1,2:T(8,128)(2,1)} %get-tuple-element.334), channel_id=1, source_target_pairs={{0,1},{1,2},{2,3},{3,4},{4,5},{5,6},{6,7},{7,8},{8,9},{9,10},{10,1... | collective-permute-start | bytes 1572872 | tf_op jit(solution)/shard_map/ppermute | solution.py:41
  (65 other events, 121.0 us)
Sparse Core Ops, SparseCore 0:
  55.8 269.2 all-reduce.13
  956.7 175.5 all-reduce.15
where the time goes:
time: 1450 us; the launch traced here: 1440 us
  blocking collectives  538 us (37%)
  waiting for transfers between devices  353 us (24%)
  local copies, waits for them, and re-layouts  289 us (20%)
  matrix products  154 us (11%)
  other arithmetic  53.4 us (4%)
  starting transfers between devices  37.3 us (3%)
  between operations  14.9 us (1%)
    pmax x1, blocking collectives, shards(): edge_top = lax.pmax(jnp.max(edge_scores, axis=2), 'seq')  249 us
    psum x1, waiting for transfers between devices, broadcast(): return lax.psum(block, axis)  206 us
    psum x1, blocking collectives, shards(): edge_dquery_sum, global_sum = lax.psum((edge_dquery, global_part), 'seq')  123 us
    psum x1, blocking collectives, shards(): gain_grad = lax.psum(gain_term, ('dp', 'seq'))  106 us
    psum x1, waiting for transfers between devices, shards(): lax.psum((jnp.sum(edge_expo, axis=2), jnp.einsum('hqt,htd->hqd', edge_exp...  99.2 us
    psum x1, blocking collectives, shards(): lax.psum((jnp.sum(edge_expo, axis=2), jnp.einsum('hqt,htd->hqd', edge_exp...  59.2 us
    while x160, local copies, waits for them, and re-layouts  46.8 us
    dot_general x24, matrix products, spread_terms(): jnp.einsum('hpbc,hpbd->hpcd', coef_blocks[:, :, :, NG + offset], rows_in,...  41.4 us
  transfers between devices with their start and end apart: 9, of which 5 were waited for; matrix products, arithmetic and copies ran while one was open for 7% of the time, Pallas kernels for 0%

commit v1 on v0

--- a/solution.py
+++ b/solution.py
@@ -1,3 +1,4 @@
+import functools
 import math
 import jax
 import jax.numpy as jnp
@@ -11,6 +12,13 @@
 NR = 3
 NK = 8
 NEGATIVE = -1e30
+
+
+def bind_spans(my_tile, axis_name, dev_axis):
+    return lax.psum(lax.psum(my_tile, axis_name), dev_axis)
+
+
+serve_orders = functools.partial(bind_spans, axis_name="dp", dev_axis="seq")
 
 
 def broadcast(block, axis, owner):
@@ -336,7 +344,7 @@
     gain_term = jnp.sum(key_eff_grad * to_heads(keys[0]).astype(jnp.float32), axis=(1, 2)).reshape(
         HEADS * HD
     )
-    gain_grad = lax.psum(gain_term, ("dp", "seq"))
+    gain_grad = serve_orders(gain_term)
     return (
         from_heads(attended_all),
         from_heads(dquery_all),

time: 1450 us -> 1390 us (0.959)
  the two profiles are of different devices: /device:TPU:1 before, /device:TPU:0 now
where the time goes in v1:
time: 1390 us; the launch traced here: 1370 us
  blocking collectives  496 us (36%)
  waiting for transfers between devices  332 us (24%)
  local copies, waits for them, and re-layouts  288 us (21%)
  matrix products  154 us (11%)
  other arithmetic  53.3 us (4%)
  starting transfers between devices  35.1 us (3%)
  between operations  14.9 us (1%)
    pmax x1, blocking collectives, shards(): edge_top = lax.pmax(jnp.max(edge_scores, axis=2), 'seq')  258 us
    psum x1, waiting for transfers between devices, broadcast(): return lax.psum(block, axis)  205 us
    psum x1, blocking collectives, shards(): edge_dquery_sum, global_sum = lax.psum((edge_dquery, global_part), 'seq')  153 us
    psum x1, waiting for transfers between devices, shards(): lax.psum((jnp.sum(edge_expo, axis=2), jnp.einsum('hqt,htd->hqd', edge_exp...  76.1 us
    psum x1, blocking collectives, shards(): lax.psum((jnp.sum(edge_expo, axis=2), jnp.einsum('hqt,htd->hqd', edge_exp...  72.5 us
    while x160, local copies, waits for them, and re-layouts  46.8 us
    dot_general x24, matrix products, spread_terms(): jnp.einsum('hpbc,hpbd->hpcd', coef_blocks[:, :, :, NG + offset], rows_in,...  41.3 us
    unnamed x62, local copies, waits for them, and re-layouts  34 us
  transfers between devices with their start and end apart: 9, of which 5 were waited for; matrix products, arithmetic and copies ran while one was open for 7% of the time, Pallas kernels for 0%

profile of v1, /device:TPU:0, one launch (start us, length us, event | category | flops | bytes accessed | tf_op | source)
XLA Modules:
  0.0 1374.5 jit_solution(5641926175510165412)
XLA Ops:
  11.2 9.7 all-to-all-start
  32.5 10.3 gather_fusion
  42.8 6.9 all-to-all-start.1
  66.9 25.1 %collective-permute-done = bf16[2,64,2048]{2,1,0:T(8,128)(2,1)} collective-permute-done((bf16[2,64,2048]{2,1,0:T(8,128)(2,1)}, bf16[2,64,2048]{2,1,0:T(8,128)(2,1)}, u32[]{:S(2)}, u32[]{:S(2)}) %collective-permute-start) | collective-permute-done | bytes 524320 | tf_op jit(solution)/shard_map/ppermute | solution.py:37
  92.0 23.1 %collective-permute-done.1 = bf16[2,64,2048]{2,1,0:T(8,128)(2,1)} collective-permute-done((bf16[2,64,2048]{2,1,0:T(8,128)(2,1)}, bf16[2,64,2048]{2,1,0:T(8,128)(2,1)}, u32[]{:S(2)}, u32[]{:S(2)}) %collective-permute-start.1) | collective-permute-done | bytes 524320 | tf_op jit(solution)/shard_map/ppermute | solution.py:39
  119.6 204.8 %all-reduce.15.cloned.1.call-done = bf16[4,128,2048]{2,1,0:T(8,128)(2,1)} async-done(((bf16[4,128,2048]{2,1,0:T(8,128)(2,1)}), bf16[4,128,2048]{2,1,0:T(8,128)(2,1)}) %all-reduce.15.cloned.1.call-update) | async-done | bytes 2097168 | tf_op jit(solution)/shard_map/psum | solution.py:26
  328.4 11.8 gather_fusion.1
  340.1 8.1 fusion.134
  348.2 287.8 %while.24 = (s32[]{:T(128)}, bf16[4,4,4,64,128]{4,3,2,1,0:T(8,128)(2,1)}, bf16[4,4,4,64,128]{4,3,2,1,0:T(8,128)(2,1)}, f32[4,4,2,2,64,128]{5,1,0,2,4,3:T(4,128)}...) while((s32[]{:T(128)}, ...), condition=%wide.region_14.15_spmd.clone, body=%wide.region_10.14_spmd.clone.sunk | while | flops 952370176 | bytes 142396560 | solution.py:235
  440.0 5.2 bitcast_dynamic-update-slice_fusion.6
  583.5 5.2 bitcast_dynamic-update-slice_fusion.6
  636.0 12.7 copy.168
  648.7 10.8 reshape.529
  664.4 28.8 %scatter_fusion = bf16[288,64,256]{2,1,0:T(8,128)(2,1)} fusion(bf16[288,64,256]{2,1,0:T(8,128)(2,1)} %broadcast_in_dim.167, s32[192]{0:T(256)S(1)} %bitcast.510, bf16[192,64,256]{2,1,0:T(8,128)(2,1)} %reshape.529), kind=kCustom, calls=%fused_computation.3 | custom fusion | bytes 18875136 | tf_op jit(solution)/shard_map/scatter | solution.py:302
  693.2 5.6 all-to-all-start.2
  702.7 257.8 %pmax.7 = f32[16,128]{1,0:T(8,128)S(1)} all-reduce(f32[16,128]{1,0:T(8,128)S(1)} %get-tuple-element.354), channel_id=1, replica_groups=mesh['dp'=8,'seq'=32] {'seq'}, use_global_device_ids=true, to_apply=%region_2.3 | all-reduce | flops 2048 | bytes 16384 | tf_op jit(solution)/shard_map/pmax | solution.py:259
  967.8 72.5 %psum.51 = f32[16,128]{1,0:T(8,128)S(1)} all-reduce(f32[16,128]{1,0:T(8,128)S(1)} %fusion.95), channel_id=1, replica_groups=mesh['dp'=8,'seq'=32] {'seq'}, use_global_device_ids=true, to_apply=%region_5.6 | all-reduce | flops 2048 | bytes 16384 | tf_op jit(solution)/shard_map/psum | solution.py:261
  1049.1 5.5 collective-permute-start.3
  1054.6 76.1 %all-reduce.17.cloned.1.call-done = (f32[16,128,128]{2,1,0:T(8,128)}, f32[16,2,2,64,128]{4,0,1,3,2:T(8,128)}) async-done(((f32[16,128,128]{2,1,0:T(8,128)}, f32[16,2,2,64,128]{4,0,1,3,2:T(8,128)}), (f32[16,128,128]{2,1,0:T(8,128)}, f32[16,2,2,64,128]{4,0,1,3,2:T(8,128)})) %all-reduce.17.cloned.1.call-update) | async-done | bytes 3145744 | tf_op jit(solution)/shard_map/psum | solution.py:261
  1140.5 18.9 %copy.212 = bf16[36,8,64,256]{3,1,2,0:T(8,128)(2,1)} copy(bf16[36,8,64,256]{3,2,1,0:T(8,128)(2,1)} %bitcast.182) | data formatting | bytes 18874368
  1159.3 16.0 %dot_general.116 = bf16[64,2,128,288]{2,1,0,3:T(2,128)(2,1)} reshape(bf16[16384,288]{0,1:T(8,128)(2,1)} %bitcast.459) | data formatting | bytes 18874368 | tf_op jit(solution)/shard_map/dot_general | solution.py:310
  1175.3 12.3 fusion.85
  1193.8 12.6 psum.54
  1206.4 152.7 %all-reduce.18 = (bf16[16,2,64,128]{3,2,1,0:T(8,128)(2,1)S(1)}, f32[2048]{0:T(1024)}) all-reduce(f32[16,2,64,128]{3,2,1,0:T(8,128)S(1)} %bitcast.484, f32[2048]{0:T(1024)S(1)} %psum.54), channel_id=1, replica_groups=mesh['dp'=8,'seq'=32] {'seq'}, use_global_device_ids=true, to_apply=%region_16.17 | all-reduce | flops 264192 | bytes 1589248 | tf_op jit(solution)/shard_map/psum | solution.py:320
  (481 shorter events, 365.3 us)
Async XLA Ops:
  9.3 57.4 %copy-start.33 = (s32[192,1]{0,1:T(1,128)}, s32[192,1]{0,1:T(1,128)S(1)}, u32[]{:S(2)}) copy-start(s32[192,1]{0,1:T(1,128)S(1)} %compare_select_fusion.1) | copy-start | bytes 2308
  11.2 19.4 %all-to-all-start = ((s32[32,1,9]{2,1,0:T(1,128)}), s32[32,1,9]{2,1,0:T(1,128)S(1)}, u32[]{:S(2)}, u32[]{:S(2)}) async-start(s32[32,1,9]{2,1,0:T(1,128)} %bitcast.20), calls=%async_computation | async-start | bytes 32768 | tf_op jit(solution)/shard_map/all_to_all | solution.py:190
  42.8 285.6 %all-to-all-start.1 = ((bf16[32,9,64,256]{3,2,1,0:T(8,128)(2,1)}), bf16[32,9,64,256]{3,2,1,0:T(8,128)(2,1)}, u32[]{:S(2)}, u32[]{:S(2)}) async-start(bf16[32,9,64,256]{3,2,1,0:T(8,128)(2,1)} %bitcast.458), calls=%async_computation.1 | async-start | bytes 18874368 | tf_op jit(solution)/shard_map/all_to_all | solution.py:193
  49.7 274.7 %all-reduce.15.cloned.1.call-start = ((), (), s32[]{:S(2)}) async-start(), calls=%async_computation.3 | async-start | bytes 4194304 | tf_op jit(solution)/shard_map/psum | solution.py:26
  56.2 35.7 %collective-permute-start = (bf16[2,64,2048]{2,1,0:T(8,128)(2,1)}, bf16[2,64,2048]{2,1,0:T(8,128)(2,1)}, u32[]{:S(2)}, u32[]{:S(2)}) collective-permute-start(bf16[2,64,2048]{2,1,0:T(8,128)(2,1)} %get-tuple-element.344), channel_id=1, source_target_pairs={{0,1},{1,2},{2,3},{3,4},{4,5},{5,6},{6,7},{7,8},{8,9},{9,10},{10,1... | collective-permute-start | bytes 1572872 | tf_op jit(solution)/shard_map/ppermute | solution.py:37
  60.6 54.4 %collective-permute-start.1 = (bf16[2,64,2048]{2,1,0:T(8,128)(2,1)}, bf16[2,64,2048]{2,1,0:T(8,128)(2,1)}, u32[]{:S(2)}, u32[]{:S(2)}) collective-permute-start(bf16[2,64,2048]{2,1,0:T(8,128)(2,1)} %get-tuple-element.345), channel_id=1, source_target_pairs={{1,0},{2,1},{3,2},{4,3},{5,4},{6,5},{7,6},{8,7},{9,8},{10,9},{11,1... | collective-permute-start | bytes 1572872 | tf_op jit(solution)/shard_map/ppermute | solution.py:39
  355.5 3.7 copy-start.1
  379.8 3.8 copy-start.5
  427.3 3.7 copy-start.1
  451.6 3.8 copy-start.5
  499.0 3.7 copy-start.1
  523.3 3.8 copy-start.5
  570.8 3.7 copy-start.1
  595.1 3.8 copy-start.5
  659.5 4.9 copy-start.34
  693.2 5.7 copy-start.7
  693.2 5.7 copy-start.31
  693.2 447.3 %all-to-all-start.2 = ((bf16[32,9,64,256]{3,2,1,0:T(8,128)(2,1)}), bf16[32,9,64,256]{3,2,1,0:T(8,128)(2,1)}, u32[]{:S(2)}, u32[]{:S(2)}) async-start(bf16[32,9,64,256]{3,2,1,0:T(8,128)(2,1)} %bitcast.456), calls=%async_computation.2 | async-start | bytes 18874368 | tf_op jit(solution)/shard_map/all_to_all | solution.py:305
  698.8 432.0 %all-reduce.17.cloned.1.call-start = ((), (), s32[]{:S(2)}) async-start(), calls=%async_computation.4 | async-start | bytes 6291456 | tf_op jit(solution)/shard_map/psum | solution.py:261
  1040.4 5.5 slice-start.1
  1040.4 5.5 slice-start.2
  1047.8 139.8 %collective-permute-start.2 = (bf16[16,2,64,128]{3,0,1,2:T(8,128)(2,1)}, bf16[16,2,64,128]{3,0,1,2:T(8,128)(2,1)}, u32[]{:S(2)}, u32[]{:S(2)}) collective-permute-start(bf16[16,2,64,128]{3,0,1,2:T(8,128)(2,1)} %get-tuple-element.337), channel_id=1, source_target_pairs={{1,0},{2,1},{3,2},{4,3},{5,4},{6,5},{7,6},{8,7},{9,8},{10,9},{11,1... | collective-permute-start | bytes 1572872 | tf_op jit(solution)/shard_map/ppermute | solution.py:49
  1049.1 140.0 %collective-permute-start.3 = (bf16[16,2,64,128]{3,0,1,2:T(8,128)(2,1)}, bf16[16,2,64,128]{3,0,1,2:T(8,128)(2,1)}, u32[]{:S(2)}, u32[]{:S(2)}) collective-permute-start(bf16[16,2,64,128]{3,0,1,2:T(8,128)(2,1)} %get-tuple-element.336), channel_id=1, source_target_pairs={{0,1},{1,2},{2,3},{3,4},{4,5},{5,6},{6,7},{7,8},{8,9},{9,10},{10,1... | collective-permute-start | bytes 1572872 | tf_op jit(solution)/shard_map/ppermute | solution.py:49
  1192.4 14.1 %copy-start.18 = (f32[16,128,128]{2,1,0:T(8,128)S(1)}, f32[16,128,128]{2,1,0:T(8,128)}, u32[]{:S(2)}) copy-start(f32[16,128,128]{2,1,0:T(8,128)} %fusion.110) | copy-start | bytes 3145732
  (67 other events, 127.1 us)
Sparse Core Ops, SparseCore 0:
  54.1 270.2 all-reduce.14
  964.2 166.5 all-reduce.16
